TPU v7x, 32 devices: a whole 2x2x4 slice. The times are simulated.
32 devices in a mesh: vocab: 8 (over z, y), batch: 4 (over x, core).
Axes of the slice: x: 2, y: 2, z: 4, core: 2. Of those that a mesh axis runs over, the one named last changes fastest.
Arguments:
- latent_activation: bfloat16 [3, 512, 6144], P(None, ('batch', 'vocab')), parts along dimension 1, may hold values from -6 to 6
- readout_matrix: bfloat16 [6144, 32768], P(None, 'vocab'), may hold values from -0.078125 to 0.078125
- caller_additive_shift: float32 [512, 32768], P('batch', 'vocab'), parts along dimension 0, may hold values from -4 to 600
- uniform_jitter: float32 [3, 512, 32768], P(None, 'batch', 'vocab'), parts along dimension 1, may hold values from 0.001 to 0.999
- context_word_indices: int32 [512, 256], P('batch'), parts along dimension 0, may hold values from 0 to 32767
- emitted_word_indices: int32 [512, 3], P('batch'), parts along dimension 0, may hold values from 0 to 32767
- heat_factor: float32 [512], P('batch'), parts along dimension 0, may hold values from 0.7 to 1.4
- recurrence_charge: float32 [512], P('batch'), parts along dimension 0, may hold values from 1.05 to 1.3
- appearance_charge: float32 [512], P('batch'), parts along dimension 0, may hold values from 0 to 1
- occurrence_charge: float32 [512], P('batch'), parts along dimension 0, may hold values from 0 to 1
Outputs:
- perturbed_max: float32 [3, 512], P(None, 'batch'), parts along dimension 1
- target_logprob: float32 [3, 512], P(None, 'batch'), parts along dimension 1
- last_logprobs: float32 [512, 32768], P('batch', 'vocab'), parts along dimension 0
There are 4 independent parts, one for each index of `batch`. A program takes and returns all parts, laid end to end along the dimension named above; an argument that names none is the same for every part. Nothing has to cross between parts.
All inputs are finite; a program needn't handle non-finite values.
Results may differ from a plain program's by a relative error of at most 0.0003.
Values may be sent and summed in bfloat16 or wider, within the bound.
A program may use at most 128 MiB of HBM per device.

v0:
```python
import math

import jax
import jax.numpy as jnp
from jax import lax
from jax.sharding import PartitionSpec as P


def count_prompt(context_word_indices, vocab_ids):
    batch_rows, length = context_word_indices.shape
    block_size = math.gcd(length, 32)

    def add_block(turn_index, totals):
        id_block = lax.dynamic_slice_in_dim(
            context_word_indices, turn_index * block_size, block_size, 1
        )
        matches = (id_block[:, :, None] == vocab_ids[None, None, :]).astype(jnp.int32)
        return totals + jnp.sum(matches, axis=1)

    empty = jnp.zeros((batch_rows, vocab_ids.shape[0]), jnp.int32)
    return lax.fori_loop(0, length // block_size, add_block, empty)


def enforce_repeat_charges(
    plain_energies,
    word_tallies,
    caller_additive_shift,
    soften_by_heat,
    repeat,
    appearance_charge,
    occurrence_charge,
):
    seen = word_tallies > 0
    counted = word_tallies.astype(jnp.float32)
    biased = plain_energies + caller_additive_shift
    cooled_energies = jnp.where(
        seen, jnp.where(biased > 0, biased / repeat, biased * repeat), biased
    )
    cooled_energies = (
        cooled_energies - occurrence_charge * counted - appearance_charge * seen.astype(jnp.float32)
    )
    return cooled_energies / soften_by_heat


def summarize(word_energies, gumbel, target_hit):
    local_top = jnp.max(word_energies, axis=-1)
    perturbed = jnp.max(word_energies + gumbel, axis=-1)
    target_score = jnp.sum(jnp.where(target_hit, word_energies, 0.0), axis=-1)
    top, best = lax.pmax((local_top, perturbed), "vocab")
    local_sum = jnp.sum(jnp.exp(word_energies - top[..., None]), axis=-1)
    total, target_total = lax.psum((local_sum, target_score), "vocab")
    normalizer = top + jnp.log(total)
    return (best, target_total - normalizer, normalizer)


def per_device(
    latent_activation,
    readout_matrix,
    caller_additive_shift,
    uniform_jitter,
    context_word_indices,
    emitted_word_indices,
    heat_factor,
    recurrence_charge,
    appearance_charge,
    occurrence_charge,
):
    width = readout_matrix.shape[1]
    vocab_ids = lax.axis_index("vocab") * width + jnp.arange(width, dtype=jnp.int32)
    prompt_counts = count_prompt(context_word_indices, vocab_ids)
    hits = (jnp.transpose(emitted_word_indices)[:, :, None] == vocab_ids[None, None, :]).astype(
        jnp.int32
    )
    soften_by_heat = heat_factor[:, None]
    repeat = recurrence_charge[:, None]
    present = appearance_charge[:, None]
    frequent = occurrence_charge[:, None]
    gumbel_all = -jnp.log(-jnp.log(uniform_jitter))
    plain_energies = jnp.einsum(
        "sbd,dv->sbv",
        lax.all_gather(latent_activation, "vocab", axis=1, tiled=True),
        readout_matrix,
        preferred_element_type=jnp.float32,
    )
    word_tallies = prompt_counts[None] + jnp.cumsum(hits, axis=0) - hits
    word_energies = enforce_repeat_charges(
        plain_energies,
        word_tallies,
        caller_additive_shift,
        soften_by_heat,
        repeat,
        present,
        frequent,
    )
    best, target_logprob, normalizer = summarize(word_energies, gumbel_all, hits > 0)
    last = word_energies[-1] - normalizer[-1][:, None]
    return (best, target_logprob, last)


def solution(mesh):
    in_specs = (
        P(None, ("batch", "vocab"), None),
        P(None, "vocab"),
        P("batch", "vocab"),
        P(None, "batch", "vocab"),
        P("batch", None),
        P("batch", None),
        P("batch"),
        P("batch"),
        P("batch"),
        P("batch"),
    )
    out_specs = (P(None, "batch"), P(None, "batch"), P("batch", "vocab"))
    return jax.shard_map(
        per_device, mesh=mesh, in_specs=in_specs, out_specs=out_specs, check_vma=False
    )
```

profile of v0, /device:TPU:0, one launch (start us, length us, event | category | flops | bytes accessed | tf_op | source)
XLA Modules:
  0.0 222.9 jit_solution(7431095952848342169)
XLA Ops:
  7.9 104.6 %while.14 = (s32[]{:T(128)}, s32[128,4096]{1,0:T(8,128)S(1)}, s32[128,256]{1,0:T(8,128)}, s32[]{:T(128)}, s32[]{:T(128)}, /*index=5*/s32[]{:T(128)}, s32[]{:T(128)}, s32[]{:T(128)}) while((s32[]{:T(128)}, s32[128,4096]{1,0:T(8,128)S(1)}, s32[128,256]{1,0:T(8,128)}, s32[]{:T(128)}, s32[]{:T(128)}, /*index=5*/s32[]{:T(128)}, ...), condition=%wide.region_2.0_spmd.clone, body=%wide.region_0.0_spmd.clone.sunk | while | flops 50860036 | bytes 8470685 | solution.py:21
  8.0 0.9 constant_dynamic-slice_fusion.2
  8.9 11.4 %convert_reduce_fusion.2 = s32[128,4096]{1,0:T(8,128)S(1)} fusion(s32[4096]{0:T(1024)S(1)} %iota_add_fusion.3, s32[128,32]{1,0:T(8,128)S(1)} %constant_dynamic-slice_fusion.2), kind=kLoop, calls=%fused_computation.1.clone.1 | loop fusion | flops 49807360 | bytes 2129920 | tf_op jit(solution)/shard_map/while/body/eval_jaxpr/reduce_sum | solution.py:18
  20.3 0.7 select_add_fusion.2
  21.0 0.9 constant_dynamic-slice_fusion.2
  21.9 11.4 %convert_reduce_fusion.2 = s32[128,4096]{1,0:T(8,128)S(1)} fusion(s32[4096]{0:T(1024)S(1)} %iota_add_fusion.3, s32[128,32]{1,0:T(8,128)S(1)} %constant_dynamic-slice_fusion.2), kind=kLoop, calls=%fused_computation.1.clone.1 | loop fusion | flops 49807360 | bytes 2129920 | tf_op jit(solution)/shard_map/while/body/eval_jaxpr/reduce_sum | solution.py:18
  33.4 0.7 select_add_fusion.2
  34.1 0.9 constant_dynamic-slice_fusion.2
  35.0 11.4 %convert_reduce_fusion.2 = s32[128,4096]{1,0:T(8,128)S(1)} fusion(s32[4096]{0:T(1024)S(1)} %iota_add_fusion.3, s32[128,32]{1,0:T(8,128)S(1)} %constant_dynamic-slice_fusion.2), kind=kLoop, calls=%fused_computation.1.clone.1 | loop fusion | flops 49807360 | bytes 2129920 | tf_op jit(solution)/shard_map/while/body/eval_jaxpr/reduce_sum | solution.py:18
  46.4 0.7 select_add_fusion.2
  47.2 0.9 constant_dynamic-slice_fusion.2
  48.1 11.4 %convert_reduce_fusion.2 = s32[128,4096]{1,0:T(8,128)S(1)} fusion(s32[4096]{0:T(1024)S(1)} %iota_add_fusion.3, s32[128,32]{1,0:T(8,128)S(1)} %constant_dynamic-slice_fusion.2), kind=kLoop, calls=%fused_computation.1.clone.1 | loop fusion | flops 49807360 | bytes 2129920 | tf_op jit(solution)/shard_map/while/body/eval_jaxpr/reduce_sum | solution.py:18
  59.5 0.7 select_add_fusion.2
  60.3 0.9 constant_dynamic-slice_fusion.2
  61.2 11.4 %convert_reduce_fusion.2 = s32[128,4096]{1,0:T(8,128)S(1)} fusion(s32[4096]{0:T(1024)S(1)} %iota_add_fusion.3, s32[128,32]{1,0:T(8,128)S(1)} %constant_dynamic-slice_fusion.2), kind=kLoop, calls=%fused_computation.1.clone.1 | loop fusion | flops 49807360 | bytes 2129920 | tf_op jit(solution)/shard_map/while/body/eval_jaxpr/reduce_sum | solution.py:18
  72.6 0.7 select_add_fusion.2
  73.3 0.9 constant_dynamic-slice_fusion.2
  74.2 11.4 %convert_reduce_fusion.2 = s32[128,4096]{1,0:T(8,128)S(1)} fusion(s32[4096]{0:T(1024)S(1)} %iota_add_fusion.3, s32[128,32]{1,0:T(8,128)S(1)} %constant_dynamic-slice_fusion.2), kind=kLoop, calls=%fused_computation.1.clone.1 | loop fusion | flops 49807360 | bytes 2129920 | tf_op jit(solution)/shard_map/while/body/eval_jaxpr/reduce_sum | solution.py:18
  85.7 0.7 select_add_fusion.2
  86.4 0.9 constant_dynamic-slice_fusion.2
  87.3 11.4 %convert_reduce_fusion.2 = s32[128,4096]{1,0:T(8,128)S(1)} fusion(s32[4096]{0:T(1024)S(1)} %iota_add_fusion.3, s32[128,32]{1,0:T(8,128)S(1)} %constant_dynamic-slice_fusion.2), kind=kLoop, calls=%fused_computation.1.clone.1 | loop fusion | flops 49807360 | bytes 2129920 | tf_op jit(solution)/shard_map/while/body/eval_jaxpr/reduce_sum | solution.py:18
  98.7 0.7 select_add_fusion.2
  99.5 0.9 constant_dynamic-slice_fusion.2
  100.4 11.4 %convert_reduce_fusion.2 = s32[128,4096]{1,0:T(8,128)S(1)} fusion(s32[4096]{0:T(1024)S(1)} %iota_add_fusion.3, s32[128,32]{1,0:T(8,128)S(1)} %constant_dynamic-slice_fusion.2), kind=kLoop, calls=%fused_computation.1.clone.1 | loop fusion | flops 49807360 | bytes 2129920 | tf_op jit(solution)/shard_map/while/body/eval_jaxpr/reduce_sum | solution.py:18
  111.8 0.7 select_add_fusion.2
  112.6 26.2 %fusion.2 = f32[3,128,4096]{2,1,0:T(8,128)S(1)} fusion(bf16[3,128,6144]{2,1,0:T(8,128)(2,1)} %all-gather.2.cloned.1.call-done, bf16[6144,4096]{1,0:T(8,128)(2,1)} %param.13), kind=kOutput, calls=%fused_computation.5 | convolution fusion | flops 19327352832 | bytes 61341696 | tf_op jit(solution)/shard_map/sbd,dv->sbv/dot_general | solution.py:79
  138.9 7.2 %fusion.18 = (f32[3,128]{1,0:T(4,128)S(1)}, f32[3,128,4096]{2,1,0:T(8,128)}) fusion(f32[128]{0:T(128)S(1)} %copy-done.2, f32[128]{0:T(128)S(1)} %copy-done.3, f32[128]{0:T(128)S(1)} %copy-done.4, f32[128]{0:T(128)S(1)} %copy-done.5, f32[3,128,4096]{2,1,0:T(8,128)S(1)} %fusion.2, f32[128,4096]{1,0:T(8,128)S(1)} %copy-done, s32[4096]{0:T(1024)S(1)} %iota_add_fusion.1, ...), kind=kOutput, calls=%fused_computation.25 | output fusion | flops 34602624 | bytes 16798720 | tf_op jit(solution)/shard_map/jit(cumsum)/reduce_window_sum | solution.py:85
  146.2 23.2 %pmax.15 = f32[3,128]{1,0:T(4,128)S(1)} all-reduce(f32[3,128]{1,0:T(4,128)S(1)} %get-tuple-element.116), channel_id=1, replica_groups=mesh['vocab'=8,'batch'=4] {'vocab'}, use_global_device_ids=true, to_apply=%region_9.10 | all-reduce | flops 384 | bytes 3072 | tf_op jit(solution)/shard_map/pmax | solution.py:49
  169.3 6.2 %exponential_reduce_fusion = (f32[3,128]{1,0:T(4,128)S(1)}, f32[3,128]{1,0:T(4,128)S(1)}, f32[3,128]{1,0:T(4,128)S(1)}) fusion(f32[3,128,4096]{2,1,0:T(8,128)} %get-tuple-element.117, f32[3,128]{1,0:T(4,128)S(1)} %pmax.15, s32[4096]{0:T(1024)S(1)} %iota_add_fusion.1, s32[3,128]{1,0:T(4,128)S(1)} %bitcast.12, f32[3,128,4096]{2,1,0:T(8,128)} %param.15), kind=kLoop, calls=%fused_computation.13 | loop fusion | flops 17300352 | bytes 12606976 | tf_op jit(solution)/shard_map/reduce_sum | solution.py:50
  175.5 17.1 %all-reduce = (f32[3,128]{1,0:T(4,128)S(1)}, f32[3,128]{1,0:T(4,128)S(1)}) all-reduce(f32[3,128]{1,0:T(4,128)S(1)} %get-tuple-element.102, f32[3,128]{1,0:T(4,128)S(1)} %get-tuple-element.101), channel_id=1, replica_groups=mesh['vocab'=8,'batch'=4] {'vocab'}, use_global_device_ids=true, to_apply=%region_7.8 | all-reduce | flops 768 | bytes 6144 | tf_op jit(solution)/shard_map/psum | solution.py:51
  193.2 3.2 %fusion.16 = f32[128,4096]{1,0:T(8,128)} fusion(f32[3,128,4096]{2,1,0:T(8,128)} %get-tuple-element.117, f32[128]{0:T(128)S(1)} %slice_bitcast_fusion.1), kind=kLoop, calls=%fused_computation.20 | loop fusion | flops 524288 | bytes 4194816 | tf_op jit(solution)/shard_map/sub | solution.py:96
  196.4 19.7 %pmax.14 = f32[3,128]{1,0:T(4,128)} all-reduce(f32[3,128]{1,0:T(4,128)S(1)} %get-tuple-element.103), channel_id=1, replica_groups=mesh['vocab'=8,'batch'=4] {'vocab'}, use_global_device_ids=true, to_apply=%region_5.6 | all-reduce | flops 384 | bytes 3072 | tf_op jit(solution)/shard_map/pmax | solution.py:49
  (27 shorter events, 1.4 us)
Async XLA Ops:
  7.2 105.5 %all-gather.2.cloned.1.call-start = ((), (), s32[]{:S(2)}) async-start(), calls=%async_computation | async-start | bytes 5308416 | tf_op jit(solution)/shard_map/all_gather | solution.py:81
  112.5 26.4 %copy-start.1 = (s32[128,3]{0,1:T(4,128)S(1)}, s32[128,3]{0,1:T(4,128)}, u32[]{:S(2)}) copy-start(s32[128,3]{0,1:T(4,128)} %param.17) | copy-start | bytes 4612
  112.5 26.4 %copy-start.2 = (f32[128]{0:T(128)S(1)}, f32[128]{0:T(128)}, u32[]{:S(2)}) copy-start(f32[128]{0:T(128)} %param.18) | copy-start | bytes 1540
  112.6 26.3 %copy-start.3 = (f32[128]{0:T(128)S(1)}, f32[128]{0:T(128)}, u32[]{:S(2)}) copy-start(f32[128]{0:T(128)} %param.20) | copy-start | bytes 1540
  112.6 26.3 %copy-start.4 = (f32[128]{0:T(128)S(1)}, f32[128]{0:T(128)}, u32[]{:S(2)}) copy-start(f32[128]{0:T(128)} %param.21) | copy-start | bytes 1540
  112.6 26.3 %copy-start.5 = (f32[128]{0:T(128)S(1)}, f32[128]{0:T(128)}, u32[]{:S(2)}) copy-start(f32[128]{0:T(128)} %param.19) | copy-start | bytes 1540
  112.6 26.3 %copy-start = (f32[128,4096]{1,0:T(8,128)S(1)}, f32[128,4096]{1,0:T(8,128)}, u32[]{:S(2)}) copy-start(f32[128,4096]{1,0:T(8,128)} %param.14) | copy-start | bytes 6291460
Sparse Core Ops, SparseCore 0:
  10.2 82.0 all-gather.1
where the time goes:
time: 223 us
  other arithmetic  114 us (51%)
  blocking collectives  60 us (27%)
  matrix products  26.2 us (12%)
  between operations  14.2 us (6%)
  local copies, waits for them, and re-layouts  7.43 us (3%)
    reduce_sum x8, other arithmetic, add_block(): return totals + jnp.sum(matches, axis=1)  91.3 us
    pmax x2, blocking collectives, summarize(): top, best = lax.pmax((local_top, perturbed), 'vocab')  42.8 us
    dot_general x1, matrix products, per_device(): jnp.einsum('sbd,dv->sbv', lax.all_gather(latent_activation, 'vocab', axis...  26.2 us
    psum x1, blocking collectives, summarize(): total, target_total = lax.psum((local_sum, target_score), 'vocab')  17.1 us
    dynamic_slice x8, local copies, waits for them, and re-layouts, add_block(): lax.dynamic_slice_in_dim(context_word_indices, turn_index * block_size, b...  7.38 us
    another operation x1, other arithmetic, per_device(): word_tallies = prompt_counts[None] + jnp.cumsum(hits, axis=0) - hits  7.23 us
    reduce_sum x1, other arithmetic, summarize(): local_sum = jnp.sum(jnp.exp(word_energies - top[..., None]), axis=-1)  6.17 us
    add x8, other arithmetic, add_block(): return totals + jnp.sum(matches, axis=1)  5.5 us
  transfers between devices with their start and end apart: 1, of which 0 were waited for; matrix products, arithmetic and copies ran while one was open for 47% of the time, Pallas kernels for 0%

commit v1 on v0

--- a/solution.py
+++ b/solution.py
@@ -1,9 +1,19 @@
+import functools
 import math
 
 import jax
 import jax.numpy as jnp
 from jax import lax
+from jax.experimental import pallas as pl
+from jax.experimental.pallas import tpu as pltpu
 from jax.sharding import PartitionSpec as P
+
+MESH = pl.DeviceIdType.MESH
+LANES = 128
+AHEAD = 2
+SLOTS = 4
+DOT_COLUMNS = 512
+TAIL_COLUMNS = 512
 
 
 def count_prompt(context_word_indices, vocab_ids):
@@ -97,6 +107,453 @@
     return (best, target_logprob, last)
 
 
+def fused_kernel(
+    n,
+    chunks,
+    x_hbm,
+    w_hbm,
+    shift_hbm,
+    u_hbm,
+    ids_ref,
+    emitted_ref,
+    heat_ref,
+    repeat_ref,
+    appear_ref,
+    occur_ref,
+    scores_hbm,
+    stats_out,
+    xg,
+    wbuf,
+    acc,
+    gumbel,
+    shift,
+    counts,
+    tally,
+    last,
+    params,
+    stats,
+    exchange,
+    own_sem,
+    w_sem,
+    in_sem,
+    out_sem,
+    send_sem,
+    recv_sem,
+    ex_send,
+    ex_recv,
+):
+    steps, rows, _ = x_hbm.shape
+    batch, width = shift_hbm.shape
+    length = ids_ref.shape[1]
+    depth = w_hbm.shape[0] // chunks
+    high = width // LANES
+    slab = steps * rows
+    levels = n // 2
+    me = lax.axis_index("vocab")
+    z = me // 2
+    y = lax.rem(me, 2)
+    twin = z * 2 + (1 - y)
+
+    u_copy = pltpu.make_async_copy(u_hbm, gumbel, in_sem.at[0])
+    shift_copy = pltpu.make_async_copy(shift_hbm, shift, in_sem.at[1])
+
+    def own_copy(chunk, t):
+        return pltpu.make_async_copy(
+            x_hbm.at[t, :, pl.ds(pl.multiple_of(chunk * depth, depth), depth)],
+            xg.at[chunk, me, pl.ds(t * rows, rows), :],
+            own_sem.at[chunk, t],
+        )
+
+    def w_copy(chunk):
+        slot = lax.rem(chunk, SLOTS)
+        return pltpu.make_async_copy(
+            w_hbm.at[pl.ds(pl.multiple_of(chunk * depth, depth), depth), :],
+            wbuf.at[slot],
+            w_sem.at[slot],
+        )
+
+    def send(source, chunk, way, target):
+        return pltpu.make_async_remote_copy(
+            src_ref=xg.at[chunk, source],
+            dst_ref=xg.at[chunk, source],
+            send_sem=send_sem.at[chunk, source, way],
+            recv_sem=recv_sem.at[chunk, source],
+            device_id={"vocab": target},
+            device_id_type=MESH,
+        )
+
+    def arrived(source, chunk):
+        send(source, chunk, 0, twin).wait_recv()
+
+    def start_own(chunk):
+        for t in range(steps):
+            own_copy(chunk, t).wait()
+        send(me, chunk, 0, twin).start()
+
+        @pl.when(z < levels - 1)
+        def _():
+            send(me, chunk, 1, me + 2).start()
+
+        @pl.when(z > 0)
+        def _():
+            send(me, chunk, 2, me - 2).start()
+
+    def relay(chunk, distance):
+        @pl.when(z >= distance)
+        def _():
+            source = me - 2 * distance
+            arrived(source, chunk)
+            send(source, chunk, 0, twin).start()
+
+            @pl.when(z < levels - 1)
+            def _():
+                send(source, chunk, 1, me + 2).start()
+
+        @pl.when(z + distance < levels)
+        def _():
+            source = me + 2 * distance
+            arrived(source, chunk)
+            send(source, chunk, 0, twin).start()
+
+            @pl.when(z > 0)
+            def _():
+                send(source, chunk, 2, me - 2).start()
+
+    for chunk in range(chunks):
+        for t in range(steps):
+            own_copy(chunk, t).start()
+    u_copy.start()
+    for chunk in range(min(SLOTS, chunks)):
+        w_copy(jnp.int32(chunk)).start()
+    shift_copy.start()
+
+    barrier = pltpu.get_barrier_semaphore()
+    for step in range(1, n):
+        pl.semaphore_signal(
+            barrier,
+            inc=1,
+            device_id={"vocab": lax.rem(me + step, n)},
+            device_id_type=MESH,
+        )
+    pl.semaphore_wait(barrier, n - 1)
+
+    for chunk in range(min(AHEAD, chunks)):
+        start_own(jnp.int32(chunk))
+
+    params[...] = jnp.zeros_like(params)
+    inverse_heat = 1.0 / heat_ref[...]
+    params[0:1, :] = inverse_heat
+    params[1:2, :] = repeat_ref[...]
+    params[2:3, :] = 1.0 / repeat_ref[...]
+    params[3:4, :] = appear_ref[...]
+    params[4:5, :] = occur_ref[...]
+    params[...] = jnp.transpose(params[...])
+
+    def clear(j, carry):
+        acc[pl.ds(pl.multiple_of(j * slab, slab), slab), :] = jnp.zeros((slab, width), jnp.float32)
+        return carry
+
+    lax.fori_loop(0, n, clear, 0)
+    u_copy.wait()
+
+    lane_rows = lax.broadcasted_iota(jnp.int32, (LANES, length), 0)
+    high_rows = lax.broadcasted_iota(jnp.int32, (high, length), 0)
+    batch_unroll = math.gcd(rows, 8)
+
+    def prepare(group):
+        base = pl.multiple_of(group * rows, rows)
+        for t in range(steps):
+            gumbel[t, pl.ds(base, rows), :] = -jnp.log(-jnp.log(gumbel[t, pl.ds(base, rows), :]))
+
+        def count(turn, carry):
+            for inner in range(batch_unroll):
+                row = turn * batch_unroll + inner
+                ids = ids_ref[pl.ds(base + row, 1), :]
+                low = jnp.bitwise_and(ids, LANES - 1)
+                top = jnp.right_shift(ids, LANES.bit_length() - 1) - me * high
+                low_hot = jnp.where(lane_rows == low, 1.0, 0.0).astype(jnp.bfloat16)
+                top_hot = jnp.where(high_rows == top, 1.0, 0.0).astype(jnp.bfloat16)
+                tally[pl.ds(pl.multiple_of(row * high, high), high), :] = lax.dot_general(
+                    top_hot,
+                    low_hot,
+                    (((1,), (1,)), ((), ())),
+                    preferred_element_type=jnp.float32,
+                )
+            return carry
+
+        lax.fori_loop(0, rows // batch_unroll, count, 0)
+        for h in range(high):
+            counts[pl.ds(base, rows), h * LANES : (h + 1) * LANES] = tally[
+                pl.ds(h, rows, stride=high), :
+            ]
+
+    def multiply(chunk):
+        w_copy(chunk).wait()
+        slot = lax.rem(chunk, SLOTS)
+
+        def tile(i, carry):
+            columns = pl.ds(pl.multiple_of(i * DOT_COLUMNS, DOT_COLUMNS), DOT_COLUMNS)
+            acc[:, columns] += jnp.dot(
+                xg[chunk].reshape(n * slab, depth),
+                wbuf[slot, :, columns],
+                preferred_element_type=jnp.float32,
+            )
+            return carry
+
+        lax.fori_loop(0, width // DOT_COLUMNS, tile, 0)
+
+        @pl.when(chunk + SLOTS < chunks)
+        def _():
+            w_copy(chunk + SLOTS).start()
+
+    def turn(i, carry):
+        @pl.when(i + AHEAD < chunks)
+        def _():
+            start_own(i + AHEAD)
+
+        for distance in range(1, levels):
+            chunk = i - (distance - 1)
+
+            @pl.when(jnp.logical_and(chunk >= 0, chunk < chunks))
+            def _():
+                relay(chunk, distance)
+
+        @pl.when(i < n)
+        def _():
+            prepare(i)
+
+        done = i - (levels - 1)
+
+        @pl.when(done >= 0)
+        def _():
+            for level in range(levels):
+                arrived(level * 2 + (1 - y), done)
+            multiply(done)
+
+        return carry
+
+    lax.fori_loop(0, max(chunks + levels - 1, n), turn, 0)
+    shift_copy.wait()
+
+    column_ids = lax.broadcasted_iota(jnp.int32, (rows, TAIL_COLUMNS), 1) + me * width
+    stat_lanes = lax.broadcasted_iota(jnp.int32, (rows, LANES), 1)
+
+    def fold(values, combine):
+        out = values[:, :LANES]
+        for k in range(1, values.shape[1] // LANES):
+            out = combine(out, values[:, k * LANES : (k + 1) * LANES])
+        return out
+
+    def finish(group, carry):
+        base = pl.multiple_of(group * rows, rows)
+        here = pl.ds(base, rows)
+        inverse_heat = params[here, 0:1]
+        repeat = params[here, 1:2]
+        inverse_repeat = params[here, 2:3]
+        appear = params[here, 3:4]
+        occur = params[here, 4:5]
+        taken = [emitted_ref[here, t : t + 1] for t in range(steps)]
+
+        def score(i, state):
+            columns = pl.ds(pl.multiple_of(i * TAIL_COLUMNS, TAIL_COLUMNS), TAIL_COLUMNS)
+            vocab_ids = column_ids + i * TAIL_COLUMNS
+            added = shift[here, columns]
+            count = counts[here, columns]
+            state = list(state)
+            for t in range(steps):
+                place = pl.ds(pl.multiple_of(group * slab + t * rows, rows), rows)
+                biased = acc[place, columns] + added
+                seen = count > 0
+                charged = biased * jnp.where(biased > 0, inverse_repeat, repeat)
+                energy = jnp.where(seen, charged - occur * count - appear, biased) * inverse_heat
+                hit = vocab_ids == taken[t]
+                acc[place, columns] = energy
+                if t == steps - 1:
+                    last[here, columns] = energy
+                state[t] = jnp.maximum(state[t], fold(energy, jnp.maximum))
+                state[steps + t] = jnp.maximum(
+                    state[steps + t], fold(energy + gumbel[t, here, columns], jnp.maximum)
+                )
+                state[2 * steps + t] += fold(jnp.where(hit, energy, 0.0), jnp.add)
+                count = count + jnp.where(hit, 1.0, 0.0)
+            return tuple(state)
+
+        lowest = jnp.full((rows, LANES), -jnp.inf, jnp.float32)
+        zero = jnp.zeros((rows, LANES), jnp.float32)
+        state = lax.fori_loop(
+            0, width // TAIL_COLUMNS, score, (lowest,) * (2 * steps) + (zero,) * steps
+        )
+        tops = [jnp.max(state[t], axis=1, keepdims=True) for t in range(steps)]
+
+        def sums(i, state):
+            columns = pl.ds(pl.multiple_of(i * TAIL_COLUMNS, TAIL_COLUMNS), TAIL_COLUMNS)
+            out = []
+            for t in range(steps):
+                place = pl.ds(pl.multiple_of(group * slab + t * rows, rows), rows)
+                out.append(state[t] + fold(jnp.exp(acc[place, columns] - tops[t]), jnp.add))
+            return tuple(out)
+
+        totals = lax.fori_loop(0, width // TAIL_COLUMNS, sums, (zero,) * steps)
+        gathered = zero
+        for t in range(steps):
+            best = jnp.max(state[steps + t], axis=1, keepdims=True)
+            target = jnp.sum(state[2 * steps + t], axis=1, keepdims=True)
+            total = jnp.sum(totals[t], axis=1, keepdims=True)
+            for k, column in enumerate((tops[t], total, best, target)):
+                gathered = jnp.where(stat_lanes == k * steps + t, column, gathered)
+        stats[here, :] = gathered
+        return carry
+
+    lax.fori_loop(0, n, finish, 0)
+    scores_copy = pltpu.make_async_copy(last, scores_hbm, out_sem.at[0])
+    scores_copy.start()
+
+    height = exchange.shape[1]
+    exchange[me] = jnp.transpose(stats[...])[:height, :]
+
+    def trade(step):
+        return pltpu.make_async_remote_copy(
+            src_ref=exchange.at[me],
+            dst_ref=exchange.at[me],
+            send_sem=ex_send.at[step],
+            recv_sem=ex_recv.at[me],
+            device_id={"vocab": lax.rem(me + step, n)},
+            device_id_type=MESH,
+        )
+
+    for step in range(1, n):
+        trade(step).start()
+
+    def wait_sends(chunk, carry):
+        send(me, chunk, 0, twin).wait_send()
+        for distance in range(levels):
+            for below in (True, False) if distance else (True,):
+                source = me - 2 * distance if below else me + 2 * distance
+                inside = z >= distance if below else z + distance < levels
+
+                @pl.when(inside)
+                def _():
+                    if distance:
+                        send(source, chunk, 0, twin).wait_send()
+                    if below:
+                        @pl.when(z < levels - 1)
+                        def _():
+                            send(source, chunk, 1, me + 2).wait_send()
+                    if not below or distance == 0:
+                        @pl.when(z > 0)
+                        def _():
+                            send(source, chunk, 2, me - 2).wait_send()
+        return carry
+
+    lax.fori_loop(0, chunks, wait_sends, 0)
+
+    for step in range(1, n):
+        other = lax.rem(me + step, n)
+        pltpu.make_async_remote_copy(
+            src_ref=exchange.at[other],
+            dst_ref=exchange.at[other],
+            send_sem=ex_send.at[step],
+            recv_sem=ex_recv.at[other],
+            device_id={"vocab": other},
+            device_id_type=MESH,
+        ).wait_recv()
+    for step in range(1, n):
+        trade(step).wait_send()
+
+    every = exchange[...]
+    tops = every[:, 0:steps, :]
+    top = jnp.max(tops, axis=0)
+    total = jnp.sum(every[:, steps : 2 * steps, :] * jnp.exp(tops - top[None]), axis=0)
+    normalizer = top + jnp.log(total)
+    stats_out[0:steps, :] = jnp.max(every[:, 2 * steps : 3 * steps, :], axis=0)
+    stats_out[steps : 2 * steps, :] = (
+        jnp.sum(every[:, 3 * steps : 4 * steps, :], axis=0) - normalizer
+    )
+    stats_out[2 * steps : 3 * steps, :] = normalizer
+    scores_copy.wait()
+
+
+def fused_device(n, chunks, *args):
+    (x, w, shift, u, ids, emitted, heat, repeat, appear, occur) = args
+    steps, rows, model = x.shape
+    batch, width = shift.shape
+    depth = model // chunks
+    high = width // LANES
+    height = -(-4 * steps // 8) * 8
+    anywhere = pl.BlockSpec(memory_space=pl.ANY)
+    inside = pl.BlockSpec(memory_space=pltpu.VMEM)
+    dma = pltpu.SemaphoreType.DMA
+    scores, stats = pl.pallas_call(
+        functools.partial(fused_kernel, n, chunks),
+        out_shape=(
+            jax.ShapeDtypeStruct((batch, width), jnp.float32),
+            jax.ShapeDtypeStruct((3 * steps, batch), jnp.float32),
+        ),
+        in_specs=[anywhere] * 4 + [inside] * 6,
+        out_specs=(anywhere, inside),
+        scratch_shapes=[
+            pltpu.VMEM((chunks, n, steps * rows, depth), x.dtype),
+            pltpu.VMEM((SLOTS, depth, width), w.dtype),
+            pltpu.VMEM((steps * batch, width), jnp.float32),
+            pltpu.VMEM((steps, batch, width), jnp.float32),
+            pltpu.VMEM((batch, width), jnp.float32),
+            pltpu.VMEM((batch, width), jnp.float32),
+            pltpu.VMEM((rows * high, LANES), jnp.float32),
+            pltpu.VMEM((batch, width), jnp.float32),
+            pltpu.VMEM((LANES, LANES), jnp.float32),
+            pltpu.VMEM((batch, LANES), jnp.float32),
+            pltpu.VMEM((n, height, batch), jnp.float32),
+            dma((chunks, steps)),
+            dma((SLOTS,)),
+            dma((2,)),
+            dma((1,)),
+            dma((chunks, n, 3)),
+            dma((chunks, n)),
+            dma((n,)),
+            dma((n,)),
+        ],
+        compiler_params=pltpu.CompilerParams(
+            collective_id=0, has_side_effects=True, vmem_limit_bytes=60 * 1024 * 1024
+        ),
+    )(
+        x,
+        w,
+        shift,
+        u,
+        ids,
+        emitted,
+        heat[None],
+        repeat[None],
+        appear[None],
+        occur[None],
+    )
+    best = stats[:steps]
+    target_logprob = stats[steps : 2 * steps]
+    return best, target_logprob, scores - stats[3 * steps - 1][:, None]
+
+
+def per_device_any(n, *args):
+    x, w, shift = args[:3]
+    steps, rows, model = x.shape
+    batch, width = shift.shape
+    chunks = 12
+    fits = (
+        n % 2 == 0
+        and n > 2
+        and rows % 16 == 0
+        and batch == LANES
+        and rows * n == batch
+        and width % max(DOT_COLUMNS, TAIL_COLUMNS) == 0
+        and (width // LANES) % 8 == 0
+        and model % (chunks * LANES) == 0
+        and args[4].shape[1] % LANES == 0
+        and 4 * steps <= LANES
+    )
+    if fits:
+        return fused_device(n, chunks, *args)
+    return per_device(*args)
+
+
 def solution(mesh):
     in_specs = (
         P(None, ("batch", "vocab"), None),
@@ -112,5 +569,6 @@
     )
     out_specs = (P(None, "batch"), P(None, "batch"), P("batch", "vocab"))
     return jax.shard_map(
-        per_device, mesh=mesh, in_specs=in_specs, out_specs=out_specs, check_vma=False
-    )
+        functools.partial(per_device_any, mesh.shape["vocab"]),
+        mesh=mesh, in_specs=in_specs, out_specs=out_specs, check_vma=False
+    )

time: 223 us -> 97.1 us (0.44)
  other arithmetic: 114 us -> 3.16 us
  Pallas kernels: 0 us -> 89.5 us
  blocking collectives: 60 us -> 0 us
  matrix products: 26.2 us -> 0 us
  between operations: 14.2 us -> 0.64 us
  local copies, waits for them, and re-layouts: 7.43 us -> 3.44 us
    reduce_sum x9 -> x0, other arithmetic: 97.5 us -> none  [the longest x8 91.3 us: add_block(): return totals + jnp.sum(matches, axis=1)]
    pallas_call x0 -> x1, Pallas kernels: none -> 89.5 us  [fused_device(): pl.pallas_call(functools.partial(fused_kernel, n, chunks), out_shape=(jax...]
    pmax x2 -> x0, blocking collectives: 42.8 us -> none  [summarize(): top, best = lax.pmax((local_top, perturbed), 'vocab')]
    dot_general x1 -> x0, matrix products: 26.2 us -> none  [per_device(): jnp.einsum('sbd,dv->sbv', lax.all_gather(latent_activation, 'vocab', axis...]
    psum x1 -> x0, blocking collectives: 17.1 us -> none  [summarize(): total, target_total = lax.psum((local_sum, target_score), 'vocab')]
    dynamic_slice x8 -> x0, local copies, waits for them, and re-layouts: 7.38 us -> none  [add_block(): lax.dynamic_slice_in_dim(context_word_indices, turn_index * block_size, b...]
    another operation x1 -> x0, other arithmetic: 7.23 us -> none  [per_device(): word_tallies = prompt_counts[None] + jnp.cumsum(hits, axis=0) - hits]
    add x17 -> x0, other arithmetic: 5.58 us -> none  [the longest x8 5.5 us: add_block(): return totals + jnp.sum(matches, axis=1)]
  transfers between devices with their start and end apart: 1 -> 0, of which waited for: 0 -> 0; matrix products, arithmetic and copies ran while one was open for 47% -> 0% of each run, Pallas kernels for 0% -> 0%
where the time goes in v1:
time: 97.1 us; the launch traced here: 96.8 us
  Pallas kernels  89.5 us (92%)
  local copies, waits for them, and re-layouts  3.44 us (4%)
  other arithmetic  3.16 us (3%)
    pallas_call x1, Pallas kernels, fused_device(): pl.pallas_call(functools.partial(fused_kernel, n, chunks), out_shape=(jax...  89.5 us
    sub x1, other arithmetic, fused_device(): return (best, target_logprob, scores - stats[3 * steps - 1][:, None])  3.16 us

profile of v1, /device:TPU:0, one launch (start us, length us, event | category | flops | bytes accessed | tf_op | source)
XLA Modules:
  0.0 96.8 jit_solution(7436772036803119476)
XLA Ops:
  0.6 1.4 %copy.13.emitted_ref = s32[128,3]{1,0:T(8,128)} copy(s32[128,3]{0,1:T(4,128)} %param.15) | data formatting | bytes 3072 | tf_op args[5]
  2.0 89.5 %shard_map.121 = (f32[128,4096]{1,0:T(8,128)}, f32[9,128]{1,0:T(8,128)}) custom-call(bf16[3,16,6144]{2,1,0:T(8,128)(2,1)} %x_hbm.1, bf16[6144,4096]{1,0:T(8,128)(2,1)} %w_hbm.1, f32[128,4096]{1,0:T(8,128)} %shift_hbm.1, f32[3,128,4096]{2,1,0:T(8,128)} %u_hbm.1, s32[128,256]{1,0:T(8,128)} %ids_ref.1, s32[128,3]{1,0:T(8,128)} %copy.13.emitted_ref, ...), custom_call_target="tpu_custom_call" | custom-call | tf_op jit(solution)/shard_map/pallas_call | solution.py:486
  91.6 1.3 %fusion = (f32[3,128]{1,0:T(4,128)}, f32[3,128]{1,0:T(4,128)}) fusion(f32[9,128]{1,0:T(8,128)} %get-tuple-element.5), kind=kLoop, calls=%fused_computation.2 | loop fusion | bytes 6144 | tf_op jit(solution)/shard_map/slice | solution.py:531
  92.9 0.7 slice_bitcast_fusion
  93.6 3.2 %broadcast_subtract_fusion = f32[128,4096]{1,0:T(8,128)} fusion(f32[128,4096]{1,0:T(8,128)} %get-tuple-element.6, f32[128]{0:T(128)S(1)} %slice_bitcast_fusion), kind=kLoop, calls=%fused_computation | loop fusion | flops 524288 | bytes 4194816 | tf_op jit(solution)/shard_map/sub | solution.py:532

commit v2 on v1

--- a/solution.py
+++ b/solution.py
@@ -10,10 +10,10 @@
 
 MESH = pl.DeviceIdType.MESH
 LANES = 128
-AHEAD = 2
-SLOTS = 4
-DOT_COLUMNS = 512
-TAIL_COLUMNS = 512
+AHEAD = 3
+SLOTS = 3
+DOT_COLUMNS = 2048
+TAIL_COLUMNS = 1024
 
 
 def count_prompt(context_word_indices, vocab_ids):
@@ -126,10 +126,11 @@
     wbuf,
     acc,
     gumbel,
-    shift,
-    counts,
+    strong,
+    weak,
+    charge,
     tally,
-    last,
+    energies,
     params,
     stats,
     exchange,
@@ -155,7 +156,13 @@
     twin = z * 2 + (1 - y)
 
     u_copy = pltpu.make_async_copy(u_hbm, gumbel, in_sem.at[0])
-    shift_copy = pltpu.make_async_copy(shift_hbm, shift, in_sem.at[1])
+
+    def shift_copy(group, t):
+        return pltpu.make_async_copy(
+            shift_hbm.at[pl.ds(group * rows, rows), :],
+            acc.at[pl.ds(group * slab + t * rows, rows), :],
+            in_sem.at[1 + group * steps + t],
+        )
 
     def own_copy(chunk, t):
         return pltpu.make_async_copy(
@@ -190,20 +197,53 @@
             own_copy(chunk, t).wait()
         send(me, chunk, 0, twin).start()
 
+        pass_along(me, chunk)
+
+    def across_first(chunk):
+        return lax.rem(chunk, 6) == 2
+
+    def pass_along(source, chunk):
         @pl.when(z < levels - 1)
         def _():
-            send(me, chunk, 1, me + 2).start()
+            send(source, chunk, 1, me + 2).start()
 
         @pl.when(z > 0)
         def _():
-            send(me, chunk, 2, me - 2).start()
+            send(source, chunk, 2, me - 2).start()
+
+    def relay_twin(chunk, distance):
+        if distance == 0:
+            arrived(twin, chunk)
+            pass_along(twin, chunk)
+            return
+
+        @pl.when(z >= distance)
+        def _():
+            source = twin - 2 * distance
+            arrived(source, chunk)
+
+            @pl.when(z < levels - 1)
+            def _():
+                send(source, chunk, 1, me + 2).start()
+
+        @pl.when(z + distance < levels)
+        def _():
+            source = twin + 2 * distance
+            arrived(source, chunk)
+
+            @pl.when(z > 0)
+            def _():
+                send(source, chunk, 2, me - 2).start()
 
     def relay(chunk, distance):
         @pl.when(z >= distance)
         def _():
             source = me - 2 * distance
             arrived(source, chunk)
-            send(source, chunk, 0, twin).start()
+
+            @pl.when(jnp.logical_not(across_first(chunk)))
+            def _():
+                send(source, chunk, 0, twin).start()
 
             @pl.when(z < levels - 1)
             def _():
@@ -213,7 +253,10 @@
         def _():
             source = me + 2 * distance
             arrived(source, chunk)
-            send(source, chunk, 0, twin).start()
+
+            @pl.when(jnp.logical_not(across_first(chunk)))
+            def _():
+                send(source, chunk, 0, twin).start()
 
             @pl.when(z > 0)
             def _():
@@ -225,7 +268,9 @@
     u_copy.start()
     for chunk in range(min(SLOTS, chunks)):
         w_copy(jnp.int32(chunk)).start()
-    shift_copy.start()
+    for group in range(n):
+        for t in range(steps):
+            shift_copy(group, t).start()
 
     barrier = pltpu.get_barrier_semaphore()
     for step in range(1, n):
@@ -243,22 +288,22 @@
     params[...] = jnp.zeros_like(params)
     inverse_heat = 1.0 / heat_ref[...]
     params[0:1, :] = inverse_heat
-    params[1:2, :] = repeat_ref[...]
-    params[2:3, :] = 1.0 / repeat_ref[...]
-    params[3:4, :] = appear_ref[...]
-    params[4:5, :] = occur_ref[...]
+    params[1:2, :] = repeat_ref[...] * inverse_heat
+    params[2:3, :] = inverse_heat / repeat_ref[...]
+    params[3:4, :] = appear_ref[...] * inverse_heat
+    params[4:5, :] = occur_ref[...] * inverse_heat
+    params[5 : 5 + steps, :] = emitted_ref[...].astype(jnp.float32)
     params[...] = jnp.transpose(params[...])
 
-    def clear(j, carry):
-        acc[pl.ds(pl.multiple_of(j * slab, slab), slab), :] = jnp.zeros((slab, width), jnp.float32)
-        return carry
-
-    lax.fori_loop(0, n, clear, 0)
     u_copy.wait()
+    for group in range(n):
+        for t in range(steps):
+            shift_copy(group, t).wait()
 
     lane_rows = lax.broadcasted_iota(jnp.int32, (LANES, length), 0)
     high_rows = lax.broadcasted_iota(jnp.int32, (high, length), 0)
     batch_unroll = math.gcd(rows, 8)
+    lane_ids = lax.broadcasted_iota(jnp.int32, (rows, LANES), 1)
 
     def prepare(group):
         base = pl.multiple_of(group * rows, rows)
@@ -282,10 +327,25 @@
             return carry
 
         lax.fori_loop(0, rows // batch_unroll, count, 0)
+        here = pl.ds(base, rows)
+        plain, repeat, inverse_repeat, appear, occur = (
+            jnp.broadcast_to(params[here, k : k + 1], (rows, LANES)) for k in range(5)
+        )
+        taken = [
+            jnp.broadcast_to(params[here, 5 + t : 6 + t], (rows, LANES)).astype(jnp.int32)
+            for t in range(steps)
+        ]
         for h in range(high):
-            counts[pl.ds(base, rows), h * LANES : (h + 1) * LANES] = tally[
-                pl.ds(h, rows, stride=high), :
-            ]
+            count = tally[pl.ds(h, rows, stride=high), :]
+            columns = slice(h * LANES, (h + 1) * LANES)
+            for t in range(steps):
+                place = pl.ds(pl.multiple_of(group * slab + t * rows, rows), rows)
+                seen = count > 0
+                strong[place, columns] = jnp.where(seen, repeat, plain)
+                weak[place, columns] = jnp.where(seen, inverse_repeat, plain)
+                charge[place, columns] = jnp.where(seen, occur * count + appear, 0.0)
+                hit = lane_ids + (me * width + h * LANES) == taken[t]
+                count = count + jnp.where(hit, 1.0, 0.0)
 
     def multiply(chunk):
         w_copy(chunk).wait()
@@ -307,17 +367,28 @@
             w_copy(chunk + SLOTS).start()
 
     def turn(i, carry):
+        for distance in reversed(range(1, levels)):
+            chunk = i - (distance - 1)
+
+            @pl.when(jnp.logical_and(chunk >= 0, chunk < chunks))
+            def _():
+                relay(chunk, distance)
+
+        for distance in reversed(range(levels - 1)):
+            chunk = i - distance
+
+            @pl.when(
+                jnp.logical_and(
+                    jnp.logical_and(chunk >= 0, chunk < chunks), across_first(chunk)
+                )
+            )
+            def _():
+                relay_twin(chunk, distance)
+
         @pl.when(i + AHEAD < chunks)
         def _():
             start_own(i + AHEAD)
 
-        for distance in range(1, levels):
-            chunk = i - (distance - 1)
-
-            @pl.when(jnp.logical_and(chunk >= 0, chunk < chunks))
-            def _():
-                relay(chunk, distance)
-
         @pl.when(i < n)
         def _():
             prepare(i)
@@ -327,55 +398,56 @@
         @pl.when(done >= 0)
         def _():
             for level in range(levels):
-                arrived(level * 2 + (1 - y), done)
+                relayed = jnp.abs(z - level) < levels - 1
+
+                @pl.when(jnp.logical_not(jnp.logical_and(across_first(done), relayed)))
+                def _():
+                    arrived(level * 2 + (1 - y), done)
+
             multiply(done)
 
         return carry
 
     lax.fori_loop(0, max(chunks + levels - 1, n), turn, 0)
-    shift_copy.wait()
-
-    column_ids = lax.broadcasted_iota(jnp.int32, (rows, TAIL_COLUMNS), 1) + me * width
-    stat_lanes = lax.broadcasted_iota(jnp.int32, (rows, LANES), 1)
-
-    def fold(values, combine):
-        out = values[:, :LANES]
-        for k in range(1, values.shape[1] // LANES):
-            out = combine(out, values[:, k * LANES : (k + 1) * LANES])
-        return out
+
+    column_ids = lane_ids + me * width
+    stat_lanes = lane_ids
+
+    def scores_copy(group):
+        top_row = pl.multiple_of(group * slab + (steps - 1) * rows, rows)
+        return pltpu.make_async_copy(
+            energies.at[pl.ds(top_row, rows), :],
+            scores_hbm.at[pl.ds(pl.multiple_of(group * rows, rows), rows), :],
+            out_sem.at[group],
+        )
 
     def finish(group, carry):
         base = pl.multiple_of(group * rows, rows)
         here = pl.ds(base, rows)
-        inverse_heat = params[here, 0:1]
-        repeat = params[here, 1:2]
-        inverse_repeat = params[here, 2:3]
-        appear = params[here, 3:4]
-        occur = params[here, 4:5]
-        taken = [emitted_ref[here, t : t + 1] for t in range(steps)]
+        taken = [
+            jnp.broadcast_to(params[here, 5 + t : 6 + t], (rows, LANES)).astype(jnp.int32)
+            for t in range(steps)
+        ]
 
         def score(i, state):
-            columns = pl.ds(pl.multiple_of(i * TAIL_COLUMNS, TAIL_COLUMNS), TAIL_COLUMNS)
-            vocab_ids = column_ids + i * TAIL_COLUMNS
-            added = shift[here, columns]
-            count = counts[here, columns]
             state = list(state)
-            for t in range(steps):
-                place = pl.ds(pl.multiple_of(group * slab + t * rows, rows), rows)
-                biased = acc[place, columns] + added
-                seen = count > 0
-                charged = biased * jnp.where(biased > 0, inverse_repeat, repeat)
-                energy = jnp.where(seen, charged - occur * count - appear, biased) * inverse_heat
-                hit = vocab_ids == taken[t]
-                acc[place, columns] = energy
-                if t == steps - 1:
-                    last[here, columns] = energy
-                state[t] = jnp.maximum(state[t], fold(energy, jnp.maximum))
-                state[steps + t] = jnp.maximum(
-                    state[steps + t], fold(energy + gumbel[t, here, columns], jnp.maximum)
-                )
-                state[2 * steps + t] += fold(jnp.where(hit, energy, 0.0), jnp.add)
-                count = count + jnp.where(hit, 1.0, 0.0)
+            for k in range(TAIL_COLUMNS // LANES):
+                start = pl.multiple_of(i * TAIL_COLUMNS + k * LANES, LANES)
+                columns = pl.ds(start, LANES)
+                vocab_ids = column_ids + start
+                for t in range(steps):
+                    place = pl.ds(pl.multiple_of(group * slab + t * rows, rows), rows)
+                    biased = acc[place, columns]
+                    energy = (
+                        jnp.minimum(biased * strong[place, columns], biased * weak[place, columns])
+                        - charge[place, columns]
+                    )
+                    energies[place, columns] = energy
+                    state[t] = jnp.maximum(state[t], energy)
+                    state[steps + t] = jnp.maximum(
+                        state[steps + t], energy + gumbel[t, here, columns]
+                    )
+                    state[2 * steps + t] += jnp.where(vocab_ids == taken[t], energy, 0.0)
             return tuple(state)
 
         lowest = jnp.full((rows, LANES), -jnp.inf, jnp.float32)
@@ -383,15 +455,19 @@
         state = lax.fori_loop(
             0, width // TAIL_COLUMNS, score, (lowest,) * (2 * steps) + (zero,) * steps
         )
+        scores_copy(group).start()
         tops = [jnp.max(state[t], axis=1, keepdims=True) for t in range(steps)]
 
+        wide_tops = [jnp.broadcast_to(top, (rows, LANES)) for top in tops]
+
         def sums(i, state):
-            columns = pl.ds(pl.multiple_of(i * TAIL_COLUMNS, TAIL_COLUMNS), TAIL_COLUMNS)
-            out = []
-            for t in range(steps):
-                place = pl.ds(pl.multiple_of(group * slab + t * rows, rows), rows)
-                out.append(state[t] + fold(jnp.exp(acc[place, columns] - tops[t]), jnp.add))
-            return tuple(out)
+            state = list(state)
+            for k in range(TAIL_COLUMNS // LANES):
+                start = pl.multiple_of(i * TAIL_COLUMNS + k * LANES, LANES)
+                for t in range(steps):
+                    place = pl.ds(pl.multiple_of(group * slab + t * rows, rows), rows)
+                    state[t] += jnp.exp(energies[place, pl.ds(start, LANES)] - wide_tops[t])
+            return tuple(state)
 
         totals = lax.fori_loop(0, width // TAIL_COLUMNS, sums, (zero,) * steps)
         gathered = zero
@@ -405,8 +481,6 @@
         return carry
 
     lax.fori_loop(0, n, finish, 0)
-    scores_copy = pltpu.make_async_copy(last, scores_hbm, out_sem.at[0])
-    scores_copy.start()
 
     height = exchange.shape[1]
     exchange[me] = jnp.transpose(stats[...])[:height, :]
@@ -425,24 +499,30 @@
         trade(step).start()
 
     def wait_sends(chunk, carry):
+        across = across_first(chunk)
         send(me, chunk, 0, twin).wait_send()
-        for distance in range(levels):
-            for below in (True, False) if distance else (True,):
-                source = me - 2 * distance if below else me + 2 * distance
-                inside = z >= distance if below else z + distance < levels
-
-                @pl.when(inside)
+        for level in range(levels):
+
+            @pl.when(jnp.logical_and(level != z, jnp.logical_not(across)))
+            def _():
+                send(level * 2 + y, chunk, 0, twin).wait_send()
+
+            @pl.when(jnp.logical_and(level <= z, z < levels - 1))
+            def _():
+                send(level * 2 + y, chunk, 1, me + 2).wait_send()
+
+                @pl.when(across)
                 def _():
-                    if distance:
-                        send(source, chunk, 0, twin).wait_send()
-                    if below:
-                        @pl.when(z < levels - 1)
-                        def _():
-                            send(source, chunk, 1, me + 2).wait_send()
-                    if not below or distance == 0:
-                        @pl.when(z > 0)
-                        def _():
-                            send(source, chunk, 2, me - 2).wait_send()
+                    send(level * 2 + 1 - y, chunk, 1, me + 2).wait_send()
+
+            @pl.when(jnp.logical_and(level >= z, z > 0))
+            def _():
+                send(level * 2 + y, chunk, 2, me - 2).wait_send()
+
+                @pl.when(across)
+                def _():
+                    send(level * 2 + 1 - y, chunk, 2, me - 2).wait_send()
+
         return carry
 
     lax.fori_loop(0, chunks, wait_sends, 0)
@@ -470,7 +550,8 @@
         jnp.sum(every[:, 3 * steps : 4 * steps, :], axis=0) - normalizer
     )
     stats_out[2 * steps : 3 * steps, :] = normalizer
-    scores_copy.wait()
+    for group in range(n):
+        scores_copy(jnp.int32(group)).wait()
 
 
 def fused_device(n, chunks, *args):
@@ -496,17 +577,18 @@
             pltpu.VMEM((SLOTS, depth, width), w.dtype),
             pltpu.VMEM((steps * batch, width), jnp.float32),
             pltpu.VMEM((steps, batch, width), jnp.float32),
-            pltpu.VMEM((batch, width), jnp.float32),
-            pltpu.VMEM((batch, width), jnp.float32),
+            pltpu.VMEM((steps * batch, width), jnp.float32),
+            pltpu.VMEM((steps * batch, width), jnp.float32),
+            pltpu.VMEM((steps * batch, width), jnp.float32),
             pltpu.VMEM((rows * high, LANES), jnp.float32),
-            pltpu.VMEM((batch, width), jnp.float32),
+            pltpu.VMEM((steps * batch, width), jnp.float32),
             pltpu.VMEM((LANES, LANES), jnp.float32),
             pltpu.VMEM((batch, LANES), jnp.float32),
             pltpu.VMEM((n, height, batch), jnp.float32),
             dma((chunks, steps)),
             dma((SLOTS,)),
-            dma((2,)),
-            dma((1,)),
+            dma((1 + n * steps,)),
+            dma((n,)),
             dma((chunks, n, 3)),
             dma((chunks, n)),
             dma((n,)),
@@ -521,7 +603,7 @@
         shift,
         u,
         ids,
-        emitted,
+        jnp.transpose(emitted),
         heat[None],
         repeat[None],
         appear[None],

time: 97.1 us -> 85.8 us (0.88)
  Pallas kernels: 89.5 us -> 79.7 us
  local copies, waits for them, and re-layouts: 3.44 us -> 2.02 us
    pallas_call x1, Pallas kernels: 89.5 us -> 79.7 us  [fused_device(): pl.pallas_call(functools.partial(fused_kernel, n, chunks), out_shape=(jax...]
    unnamed x1 -> x0, local copies, waits for them, and re-layouts: 1.42 us -> none
where the time goes in v2:
time: 85.8 us; the launch traced here: 85.5 us
  Pallas kernels  79.7 us (93%)
  other arithmetic  3.16 us (4%)
  local copies, waits for them, and re-layouts  2.02 us (2%)
    pallas_call x1, Pallas kernels, fused_device(): pl.pallas_call(functools.partial(fused_kernel, n, chunks), out_shape=(jax...  79.7 us
    sub x1, other arithmetic, fused_device(): return (best, target_logprob, scores - stats[3 * steps - 1][:, None])  3.16 us

profile of v2, /device:TPU:0, one launch (start us, length us, event | category | flops | bytes accessed | tf_op | source)
XLA Modules:
  0.0 85.5 jit_solution(3747849365248628416)
XLA Ops:
  0.6 79.7 %shard_map.121 = (f32[128,4096]{1,0:T(8,128)}, f32[9,128]{1,0:T(8,128)}) custom-call(bf16[3,16,6144]{2,1,0:T(8,128)(2,1)} %x_hbm.1, bf16[6144,4096]{1,0:T(8,128)(2,1)} %w_hbm.1, f32[128,4096]{1,0:T(8,128)} %shift_hbm.1, f32[3,128,4096]{2,1,0:T(8,128)} %u_hbm.1, s32[128,256]{1,0:T(8,128)} %ids_ref.1, s32[3,128]{1,0:T(4,128)} %bitcast.7, f32[1,128]{1,0:T(1,128)} %bitcast.8, ...), custom_call_target="tpu_custom_call" | custom-call | tf_op jit(solution)/shard_map/pallas_call | solution.py:567
  80.3 1.3 %fusion = (f32[3,128]{1,0:T(4,128)}, f32[3,128]{1,0:T(4,128)}) fusion(f32[9,128]{1,0:T(8,128)} %get-tuple-element.5), kind=kLoop, calls=%fused_computation.2 | loop fusion | bytes 6144 | tf_op jit(solution)/shard_map/slice | solution.py:613
  81.7 0.7 slice_bitcast_fusion
  82.4 3.2 %broadcast_subtract_fusion = f32[128,4096]{1,0:T(8,128)} fusion(f32[128,4096]{1,0:T(8,128)} %get-tuple-element.6, f32[128]{0:T(128)S(1)} %slice_bitcast_fusion), kind=kLoop, calls=%fused_computation | loop fusion | flops 524288 | bytes 4194816 | tf_op jit(solution)/shard_map/sub | solution.py:614

commit v3 on v2

--- a/solution.py
+++ b/solution.py
@@ -10,7 +10,7 @@
 
 MESH = pl.DeviceIdType.MESH
 LANES = 128
-AHEAD = 3
+AHEAD = 4
 SLOTS = 3
 DOT_COLUMNS = 2048
 TAIL_COLUMNS = 1024

time: 85.8 us -> 84.5 us (0.985)
  Pallas kernels: 79.7 us -> 78.5 us
    pallas_call x1, Pallas kernels: 79.7 us -> 78.5 us  [fused_device(): pl.pallas_call(functools.partial(fused_kernel, n, chunks), out_shape=(jax...]
where the time goes in v3:
time: 84.5 us; the launch traced here: 84.3 us
  Pallas kernels  78.5 us (93%)
  other arithmetic  3.16 us (4%)
  local copies, waits for them, and re-layouts  2.02 us (2%)
    pallas_call x1, Pallas kernels, fused_device(): pl.pallas_call(functools.partial(fused_kernel, n, chunks), out_shape=(jax...  78.5 us
    sub x1, other arithmetic, fused_device(): return (best, target_logprob, scores - stats[3 * steps - 1][:, None])  3.16 us

profile of v3, /device:TPU:0, one launch (start us, length us, event | category | flops | bytes accessed | tf_op | source)
XLA Modules:
  0.0 84.3 jit_solution(3058927336101561640)
XLA Ops:
  0.6 78.5 %shard_map.121 = (f32[128,4096]{1,0:T(8,128)}, f32[9,128]{1,0:T(8,128)}) custom-call(bf16[3,16,6144]{2,1,0:T(8,128)(2,1)} %x_hbm.1, bf16[6144,4096]{1,0:T(8,128)(2,1)} %w_hbm.1, f32[128,4096]{1,0:T(8,128)} %shift_hbm.1, f32[3,128,4096]{2,1,0:T(8,128)} %u_hbm.1, s32[128,256]{1,0:T(8,128)} %ids_ref.1, s32[3,128]{1,0:T(4,128)} %bitcast.7, f32[1,128]{1,0:T(1,128)} %bitcast.8, ...), custom_call_target="tpu_custom_call" | custom-call | tf_op jit(solution)/shard_map/pallas_call | solution.py:567
  79.1 1.3 %fusion = (f32[3,128]{1,0:T(4,128)}, f32[3,128]{1,0:T(4,128)}) fusion(f32[9,128]{1,0:T(8,128)} %get-tuple-element.5), kind=kLoop, calls=%fused_computation.2 | loop fusion | bytes 6144 | tf_op jit(solution)/shard_map/slice | solution.py:613
  80.4 0.7 slice_bitcast_fusion
  81.1 3.2 %broadcast_subtract_fusion = f32[128,4096]{1,0:T(8,128)} fusion(f32[128,4096]{1,0:T(8,128)} %get-tuple-element.6, f32[128]{0:T(128)S(1)} %slice_bitcast_fusion), kind=kLoop, calls=%fused_computation | loop fusion | flops 524288 | bytes 4194816 | tf_op jit(solution)/shard_map/sub | solution.py:614
